TPU v7x, 256 devices: a whole 4x4x8 slice. The times are simulated.
256 devices in a mesh: atom: 8 (over x, core), ka: 32 (over y, z).
Axes of the slice: x: 4, y: 4, z: 8, core: 2. Of those that a mesh axis runs over, the one named last changes fastest.
Arguments:
- positions: float32 [3, 131072], P(None, 'atom'), may hold values from 0 to 1
- features: bfloat16 [64, 131072], P(None, 'atom'), may hold values from -6 to 6
- species: int32 [131072], P('atom'), may hold values from 0 to 7
- miller: int32 [3, 4096], P(None, 'ka'), may hold values from -8 to 8
- species_table: float32 [64, 8], replicated, may hold values from -6 to 6
- filter_weight: float32 [64, 16], replicated, may hold values from -6 to 6
- norm_gain: float32 [64], replicated, may hold values from 0.25 to 1.75
- up_weight: bfloat16 [256, 64], replicated, may hold values from -0.75 to 0.75
- down_weight: bfloat16 [64, 256], replicated, may hold values from -0.375 to 0.375
Outputs:
- updated: bfloat16 [64, 131072], P(None, ('atom', 'ka'))
All inputs are finite; a program needn't handle non-finite values.
Results may differ from a plain program's by a relative error of at most 0.006.
Values may be sent and summed in bfloat16 or wider, within the bound.
A program may use at most 64 MiB of HBM per device.

v0:
```python
import math
import jax
import jax.numpy as jnp
from jax import lax
from jax.sharding import PartitionSpec as P

K = 4096
NRBF = 16
NSPEC = 8
two_pi = 2.0 * math.pi
k_cutoff = 14.0


def phases(coords, vectors):
    values = vectors.astype(jnp.float32)
    angles = two_pi * (
        coords[0][:, None] * values[0][None, :]
        + coords[1][:, None] * values[1][None, :]
        + coords[2][:, None] * values[2][None, :]
    )
    return (jnp.cos(angles).astype(jnp.bfloat16), jnp.sin(angles).astype(jnp.bfloat16))


def radial_filter(vectors, filter_weight):
    values = vectors.astype(jnp.float32)
    magnitude = jnp.sqrt(values[0] * values[0] + values[1] * values[1] + values[2] * values[2])
    centers = jnp.arange(NRBF, dtype=jnp.float32) * (k_cutoff / (NRBF - 1))
    basis = jnp.exp(-jnp.square((magnitude[None, :] - centers[:, None]) / (k_cutoff / NRBF)))
    return jnp.dot(
        filter_weight, basis, precision=lax.Precision.HIGHEST, preferred_element_type=jnp.float32
    )


def project_back(filtered, cosines, sines):
    dims = (((1,), (1,)), ((), ()))
    first = lax.dot_general(filtered[0], cosines, dims, preferred_element_type=jnp.float32)
    return first + lax.dot_general(filtered[1], sines, dims, preferred_element_type=jnp.float32)


def body(
    positions,
    features,
    species,
    miller,
    species_table,
    filter_weight,
    norm_gain,
    up_weight,
    down_weight,
):
    atoms_here = features.shape[1]
    local_count = atoms_here // lax.axis_size("ka")
    scaling = 1.0 / math.sqrt(atoms_here * lax.axis_size("atom") * K)
    onehot = (species[None, :] == jnp.arange(NSPEC, dtype=jnp.int32)[:, None]).astype(jnp.float32)
    embedded = jnp.dot(
        species_table, onehot, precision=lax.Precision.HIGHEST, preferred_element_type=jnp.float32
    )
    source = (features.astype(jnp.float32) + embedded).astype(jnp.bfloat16)
    cosines, sines = phases(positions, miller)
    real_part = jnp.dot(source, cosines, preferred_element_type=jnp.float32)
    imag_part = jnp.dot(source, sines, preferred_element_type=jnp.float32)
    factors = jnp.stack([real_part, imag_part])
    summed = lax.psum(factors, "atom")
    filtered = (summed * radial_filter(miller, filter_weight)[None] * scaling).astype(jnp.bfloat16)
    ka_index = lax.axis_index("ka")
    local_features = lax.dynamic_slice_in_dim(features, ka_index * local_count, local_count, 1)
    partial_sum = project_back(filtered, cosines, sines)
    message = lax.psum_scatter(partial_sum, "ka", scatter_dimension=1, tiled=True)
    mean_sq = jnp.mean(message * message, axis=0, keepdims=True)
    normed = (message * lax.rsqrt(mean_sq + 1e-06) * norm_gain[:, None]).astype(jnp.bfloat16)
    hidden = jax.nn.silu(jnp.dot(up_weight, normed, preferred_element_type=jnp.float32)).astype(
        jnp.bfloat16
    )
    update = jnp.dot(down_weight, hidden, preferred_element_type=jnp.float32)
    return (local_features.astype(jnp.float32) + update).astype(jnp.bfloat16)


def solution(mesh):
    in_specs = (P(None, "atom"), P(None, "atom"), P("atom"), P(None, "ka"), P(), P(), P(), P(), P())
    out_specs = P(None, ("atom", "ka"))
    return jax.shard_map(body, mesh=mesh, in_specs=in_specs, out_specs=out_specs, check_vma=False)
```

profile of v0, /device:TPU:2, one launch (start us, length us, event | category | flops | bytes accessed | tf_op | source)
XLA Modules:
  0.0 452.1 jit_solution(7611694238206161224)
XLA Ops:
  6.5 0.0 copy-start
  6.5 0.0 all-reduce.2.cloned.1.call-start
  6.5 0.7 convert_element_type.35
  7.2 1.5 fusion.29
  8.7 3.6 fusion.1
  12.3 30.7 %fusion.7 = f32[1,64,128]{2,1,0:T(8,128)S(1)} fusion(bf16[64,16384]{1,0:T(8,128)(2,1)S(1)} %fusion.1, f32[128]{0:T(128)S(1)} %get-tuple-element.9, f32[16384]{0:T(1024)S(1)} %bitcast.61, f32[128]{0:T(128)S(1)} %get-tuple-element.10, f32[16384]{0:T(1024)S(1)} %bitcast.65, f32[128]{0:T(128)S(1)} %get-tuple-element.11, f32[16384]{0:T(1024)S(1)} %bitcast.57), kind=kOutput, calls=%fused_computation.14 | convolution fusion | flops 283115520 | bytes 2328064 | tf_op jit(solution)/shard_map/dot_general | solution.py:60
  43.0 0.0 copy-start.2
  43.0 31.2 %fusion.8 = f32[1,64,128]{2,1,0:T(8,128)S(1)} fusion(bf16[64,16384]{1,0:T(8,128)(2,1)S(1)} %fusion.1, f32[128]{0:T(128)S(1)} %get-tuple-element.9, f32[16384]{0:T(1024)S(1)} %bitcast.62, f32[128]{0:T(128)S(1)} %get-tuple-element.10, f32[16384]{0:T(1024)S(1)} %bitcast.66, f32[128]{0:T(128)S(1)} %get-tuple-element.11, f32[16384]{0:T(1024)S(1)} %bitcast.58), kind=kOutput, calls=%fused_computation.15 | convolution fusion | flops 283115520 | bytes 2328064 | tf_op jit(solution)/shard_map/dot_general | solution.py:61
  74.2 0.6 pad_maximum_fusion
  74.9 0.0 all-reduce.2.cloned.1.call-update
  74.9 0.0 reduce-scatter.2.cloned.1.call-start
  75.0 0.0 copy-done.2
  75.0 0.2 convolution_bitcast_fusion.3
  75.2 65.4 %all-reduce.2.cloned.1.call-done = f32[2,64,128]{2,1,0:T(8,128)} async-done(((f32[2,64,128]{2,1,0:T(8,128)}), f32[2,64,128]{2,1,0:T(8,128)}) %all-reduce.2.cloned.1.call-update) | async-done | bytes 65552 | tf_op jit(solution)/shard_map/psum | solution.py:63
  140.6 0.8 multiply_convert_fusion.4
  141.5 41.2 %fusion.3 = f32[64,16384]{1,0:T(8,128)S(1)} fusion(f32[128]{0:T(128)S(1)} %get-tuple-element.9, f32[16384]{0:T(1024)S(1)} %bitcast.63, f32[128]{0:T(128)S(1)} %get-tuple-element.10, f32[16384]{0:T(1024)S(1)} %bitcast.67, f32[128]{0:T(128)S(1)} %get-tuple-element.11, f32[16384]{0:T(1024)S(1)} %bitcast.59, bf16[2,64,128]{2,1,0:T(8,128)(2,1)S(1)} %multiply_convert_fusion.4), kind=kOutput, calls=%fused_computation.8 | convolution fusion | flops 283115520 | bytes 4408832 | tf_op jit(solution)/shard_map/dot_general | solution.py:36
  182.8 34.3 %convolution_add_fusion = f32[64,16384]{1,0:T(8,128)} fusion(f32[64,16384]{1,0:T(8,128)S(1)} %fusion.3, f32[128]{0:T(128)S(1)} %get-tuple-element.9, f32[16384]{0:T(1024)S(1)} %bitcast.64, f32[128]{0:T(128)S(1)} %get-tuple-element.10, f32[16384]{0:T(1024)S(1)} %bitcast.68, f32[128]{0:T(128)S(1)} %get-tuple-element.11, f32[16384]{0:T(1024)S(1)} %bitcast.60, ...), kind=kOutput, calls=%fused_computation | convolution fusion | flops 284164096 | bytes 8603136 | tf_op jit(solution)/shard_map/dot_general | solution.py:37
  217.1 0.0 reduce-scatter.2.cloned.1.call-update
  217.1 224.9 %reduce-scatter.2.cloned.1.call-done = f32[64,512]{1,0:T(8,128)} async-done(((f32[64,16384]{1,0:T(8,128)}), f32[64,512]{1,0:T(8,128)}) %reduce-scatter.2.cloned.1.call-update) | async-done | bytes 131088 | tf_op jit(solution)/shard_map/reduce_scatter | solution.py:68
  442.0 0.9 multiply_reduce_fusion
  442.9 0.0 copy-done
  442.9 0.0 copy-done.1
  442.9 0.0 copy-done.3
  442.9 2.1 fusion.6
  (5 shorter events, 0.0 us)
Async XLA Ops:
  6.5 436.4 %copy-start = (bf16[64,256]{1,0:T(8,128)(2,1)S(1)}, bf16[64,256]{1,0:T(8,128)(2,1)}, u32[]{:S(2)}) copy-start(bf16[64,256]{1,0:T(8,128)(2,1)} %param.17) | copy-start | bytes 98308
  6.5 134.1 %all-reduce.2.cloned.1.call-start = ((), (), s32[]{:S(2)}) async-start(), calls=%async_computation.1 | async-start | bytes 131072 | tf_op jit(solution)/shard_map/psum | solution.py:63
  43.0 32.0 %copy-start.2 = (f32[64,16]{0,1:T(8,128)S(1)}, f32[64,16]{0,1:T(8,128)}, u32[]{:S(2)}) copy-start(f32[64,16]{0,1:T(8,128)} %param.14) | copy-start | bytes 12292
  74.9 367.1 %reduce-scatter.2.cloned.1.call-start = ((), (), s32[]{:S(2)}) async-start(), calls=%async_computation.2 | async-start | bytes 4325376 | tf_op jit(solution)/shard_map/reduce_scatter | solution.py:68
  217.1 225.8 %copy-start.1 = (bf16[256,64]{0,1:T(8,128)(2,1)S(1)}, bf16[256,64]{0,1:T(8,128)(2,1)}, u32[]{:S(2)}) copy-start(bf16[256,64]{0,1:T(8,128)(2,1)} %param.16) | copy-start | bytes 98308
  217.1 225.9 %copy-start.3 = (f32[64]{0:T(128)S(1)}, f32[64]{0:T(128)}, u32[]{:S(2)}) copy-start(f32[64]{0:T(128)} %param.15) | copy-start | bytes 772
Sparse Core Ops, SparseCore 0:
  75.0 65.5 all-reduce.1
  217.2 224.6 reduce-scatter.1
where the time goes:
time: 460 us; the launch traced here: 452 us
  waiting for transfers between devices  290 us (63%)
  matrix products  143 us (31%)
  between operations  13.7 us (3%)
    reduce_scatter x1, waiting for transfers between devices, body(): lax.psum_scatter(partial_sum, 'ka', scatter_dimension=1, tiled=True)  225 us
    psum x1, waiting for transfers between devices, body(): summed = lax.psum(factors, 'atom')  65.4 us
    dot_general x1, matrix products, project_back(): lax.dot_general(filtered[0], cosines, dims, preferred_element_type=jnp.fl...  41.2 us
    dot_general x1, matrix products, project_back(): lax.dot_general(filtered[1], sines, dims, preferred_element_type=jnp.floa...  34.3 us
    dot_general x1, matrix products, body(): imag_part = jnp.dot(source, sines, preferred_element_type=jnp.float32)  31.2 us
    dot_general x1, matrix products, body(): real_part = jnp.dot(source, cosines, preferred_element_type=jnp.float32)  30.7 us
  transfers between devices with their start and end apart: 2, of which 2 were waited for; matrix products, arithmetic and copies ran while one was open for 0% of the time, Pallas kernels for 0%

commit v1 on v0

--- a/solution.py
+++ b/solution.py
@@ -60,7 +60,7 @@
     real_part = jnp.dot(source, cosines, preferred_element_type=jnp.float32)
     imag_part = jnp.dot(source, sines, preferred_element_type=jnp.float32)
     factors = jnp.stack([real_part, imag_part])
-    summed = lax.psum(factors, "atom")
+    summed = jnp.sum(lax.all_gather(factors, "atom"), axis=0)
     filtered = (summed * radial_filter(miller, filter_weight)[None] * scaling).astype(jnp.bfloat16)
     ka_index = lax.axis_index("ka")
     local_features = lax.dynamic_slice_in_dim(features, ka_index * local_count, local_count, 1)

time: 460 us -> 407 us (0.88)
  waiting for transfers between devices: 290 us -> 226 us
  blocking collectives: 0 us -> 13.2 us
    psum x1 -> x0, waiting for transfers between devices: 65.4 us -> none  [body(): summed = lax.psum(factors, 'atom')]
    all_gather x0 -> x1, blocking collectives: none -> 13.2 us  [body(): summed = jnp.sum(lax.all_gather(factors, 'atom'), axis=0)]
  transfers between devices with their start and end apart: 2 -> 1, of which waited for: 2 -> 1; matrix products, arithmetic and copies ran while one was open for 0% -> 0% of each run, Pallas kernels for 0% -> 0%
where the time goes in v1:
time: 407 us; the launch traced here: 400 us
  waiting for transfers between devices  226 us (56%)
  matrix products  143 us (35%)
  between operations  13.7 us (3%)
  blocking collectives  13.2 us (3%)
    reduce_scatter x1, waiting for transfers between devices, body(): lax.psum_scatter(partial_sum, 'ka', scatter_dimension=1, tiled=True)  226 us
    dot_general x1, matrix products, project_back(): lax.dot_general(filtered[0], cosines, dims, preferred_element_type=jnp.fl...  41.2 us
    dot_general x1, matrix products, project_back(): lax.dot_general(filtered[1], sines, dims, preferred_element_type=jnp.floa...  34.3 us
    dot_general x1, matrix products, body(): imag_part = jnp.dot(source, sines, preferred_element_type=jnp.float32)  31.2 us
    dot_general x1, matrix products, body(): real_part = jnp.dot(source, cosines, preferred_element_type=jnp.float32)  30.7 us
    all_gather x1, blocking collectives, body(): summed = jnp.sum(lax.all_gather(factors, 'atom'), axis=0)  13.2 us
  transfers between devices with their start and end apart: 1, of which 1 were waited for; matrix products, arithmetic and copies ran while one was open for 0% of the time, Pallas kernels for 0%

profile of v1, /device:TPU:2, one launch (start us, length us, event | category | flops | bytes accessed | tf_op | source)
XLA Modules:
  0.0 399.6 jit_solution(1708681341135323962)
XLA Ops:
  6.5 0.0 copy-start
  6.5 0.0 reduce-scatter.2.cloned.1.call-start
  6.5 0.7 convert_element_type.35
  7.2 1.4 fusion.29
  8.6 3.6 fusion.1
  12.2 30.7 %fusion.7 = f32[1,64,128]{2,1,0:T(8,128)S(1)} fusion(bf16[64,16384]{1,0:T(8,128)(2,1)S(1)} %fusion.1, f32[128]{0:T(128)S(1)} %get-tuple-element.9, f32[16384]{0:T(1024)S(1)} %bitcast.63, f32[128]{0:T(128)S(1)} %get-tuple-element.10, f32[16384]{0:T(1024)S(1)} %bitcast.67, f32[128]{0:T(128)S(1)} %get-tuple-element.11, f32[16384]{0:T(1024)S(1)} %bitcast.59), kind=kOutput, calls=%fused_computation.14 | convolution fusion | flops 283115520 | bytes 2328064 | tf_op jit(solution)/shard_map/dot_general | solution.py:60
  42.9 0.0 copy-start.2
  42.9 31.2 %fusion.8 = f32[1,64,128]{2,1,0:T(8,128)S(1)} fusion(bf16[64,16384]{1,0:T(8,128)(2,1)S(1)} %fusion.1, f32[128]{0:T(128)S(1)} %get-tuple-element.9, f32[16384]{0:T(1024)S(1)} %bitcast.64, f32[128]{0:T(128)S(1)} %get-tuple-element.10, f32[16384]{0:T(1024)S(1)} %bitcast.68, f32[128]{0:T(128)S(1)} %get-tuple-element.11, f32[16384]{0:T(1024)S(1)} %bitcast.60), kind=kOutput, calls=%fused_computation.15 | convolution fusion | flops 283115520 | bytes 2328064 | tf_op jit(solution)/shard_map/dot_general | solution.py:61
  74.2 13.2 %all-gather = f32[16,64,128]{2,1,0:T(8,128)S(1)} all-gather(f32[2,64,128]{2,1,0:T(8,128)S(1)} %pad_maximum_fusion), channel_id=2, replica_groups=mesh['atom'=8,'ka'=32] {'atom'}, dimensions={0}, use_global_device_ids=true | all-gather | bytes 589824 | tf_op jit(solution)/shard_map/all_gather | solution.py:63
  87.4 0.0 copy-done.2
  87.4 0.2 convolution_bitcast_fusion.3
  87.6 41.2 %fusion.3 = f32[64,16384]{1,0:T(8,128)S(1)} fusion(f32[128]{0:T(128)S(1)} %get-tuple-element.9, f32[16384]{0:T(1024)S(1)} %bitcast.65, f32[128]{0:T(128)S(1)} %get-tuple-element.10, f32[16384]{0:T(1024)S(1)} %bitcast.69, f32[128]{0:T(128)S(1)} %get-tuple-element.11, f32[16384]{0:T(1024)S(1)} %bitcast.61, bf16[2,64,128]{2,1,0:T(8,128)(2,1)S(1)} %multiply_convert_fusion.4), kind=kOutput, calls=%fused_computation.8 | convolution fusion | flops 283115520 | bytes 4408832 | tf_op jit(solution)/shard_map/dot_general | solution.py:36
  128.9 34.3 %convolution_add_fusion = f32[64,16384]{1,0:T(8,128)} fusion(f32[64,16384]{1,0:T(8,128)S(1)} %fusion.3, f32[128]{0:T(128)S(1)} %get-tuple-element.9, f32[16384]{0:T(1024)S(1)} %bitcast.66, f32[128]{0:T(128)S(1)} %get-tuple-element.10, f32[16384]{0:T(1024)S(1)} %bitcast.70, f32[128]{0:T(128)S(1)} %get-tuple-element.11, f32[16384]{0:T(1024)S(1)} %bitcast.62, ...), kind=kOutput, calls=%fused_computation | convolution fusion | flops 284164096 | bytes 8603136 | tf_op jit(solution)/shard_map/dot_general | solution.py:37
  163.2 0.0 copy-start.1
  163.2 0.0 copy-start.3
  163.2 0.0 reduce-scatter.2.cloned.1.call-update
  163.3 226.3 %reduce-scatter.2.cloned.1.call-done = f32[64,512]{1,0:T(8,128)} async-done(((f32[64,16384]{1,0:T(8,128)}), f32[64,512]{1,0:T(8,128)}) %reduce-scatter.2.cloned.1.call-update) | async-done | bytes 131088 | tf_op jit(solution)/shard_map/reduce_scatter | solution.py:68
  389.5 0.9 multiply_reduce_fusion
  390.5 0.0 copy-done
  390.5 0.0 copy-done.1
  390.5 0.0 copy-done.3
  390.5 2.1 fusion.6
  (6 shorter events, 0.1 us)
Async XLA Ops:
  6.5 383.9 %copy-start = (bf16[64,256]{1,0:T(8,128)(2,1)S(1)}, bf16[64,256]{1,0:T(8,128)(2,1)}, u32[]{:S(2)}) copy-start(bf16[64,256]{1,0:T(8,128)(2,1)} %param.17) | copy-start | bytes 98308
  6.5 383.0 %reduce-scatter.2.cloned.1.call-start = ((), (), s32[]{:S(2)}) async-start(), calls=%async_computation.1 | async-start | bytes 4325376 | tf_op jit(solution)/shard_map/reduce_scatter | solution.py:68
  42.9 44.5 %copy-start.2 = (f32[64,16]{0,1:T(8,128)S(1)}, f32[64,16]{0,1:T(8,128)}, u32[]{:S(2)}) copy-start(f32[64,16]{0,1:T(8,128)} %param.14) | copy-start | bytes 12292
  163.2 227.2 %copy-start.1 = (bf16[256,64]{0,1:T(8,128)(2,1)S(1)}, bf16[256,64]{0,1:T(8,128)(2,1)}, u32[]{:S(2)}) copy-start(bf16[256,64]{0,1:T(8,128)(2,1)} %param.16) | copy-start | bytes 98308
  163.2 227.3 %copy-start.3 = (f32[64]{0:T(128)S(1)}, f32[64]{0:T(128)}, u32[]{:S(2)}) copy-start(f32[64]{0:T(128)} %param.15) | copy-start | bytes 772
Sparse Core Ops, SparseCore 0:
  163.4 226.0 reduce-scatter.1
